TPU v7x, 32 devices: a whole 2x2x4 slice. The times are simulated.
32 devices in a mesh: groups: 2 (over x), tensor: 16 (over z, y, core).
Axes of the slice: x: 2, y: 2, z: 4, core: 2. Of those that a mesh axis runs over, the one named last changes fastest.
Arguments:
- teacher_in: bfloat16 [1024, 5376], P(('groups', 'tensor')), parts along dimension 0, may hold values from -6 to 6
- gate_weight: bfloat16 [21504, 5376], P('tensor'), may hold values from -0.078125 to 0.078125
- up_weight: bfloat16 [21504, 5376], P('tensor'), may hold values from -0.078125 to 0.078125
- down_weight: bfloat16 [21504, 5376], P('tensor'), may hold values from -0.0546875 to 0.0546875
- post_gain: bfloat16 [5376], replicated, may hold values from 0.099609375 to 1.8984375
- student_in: bfloat16 [1024, 2560], P(('groups', 'tensor')), parts along dimension 0, may hold values from -6 to 6
- proj_weight: bfloat16 [5376, 2560], P('tensor'), may hold values from -0.125 to 0.125
Outputs:
- loss_value: float32 [2], P('groups'), parts along dimension 0
- proj_grad: float32 [10752, 2560], P(('groups', 'tensor')), parts along dimension 0
- student_grad: bfloat16 [1024, 2560], P(('groups', 'tensor')), parts along dimension 0
There are 2 independent parts, one for each index of `groups`. A program takes and returns all parts, laid end to end along the dimension named above; an argument that names none is the same for every part. Nothing has to cross between parts.
All inputs are finite; a program needn't handle non-finite values.
Results may differ from a plain program's by a relative error of at most 0.0051.
Values may be sent and summed in bfloat16 or wider, within the bound.
A program may use at most 128 MiB of HBM per device.

v0:
```python
import jax
import jax.numpy as jnp
from jax import lax
from jax.sharding import PartitionSpec as P

epsilon = 1e-06


def local(teacher_in, gate_weight, up_weight, down_weight, post_gain, student_in, proj_weight):
    width_count = lax.axis_size("tensor")
    gains = post_gain.astype(jnp.float32)
    contract_last = (((1,), (1,)), ((), ()))
    block_rows = lax.all_gather(teacher_in, "tensor", axis=0, tiled=True)
    gate_value = lax.dot_general(
        block_rows, gate_weight, contract_last, preferred_element_type=jnp.float32
    )
    lift_value = lax.dot_general(
        block_rows, up_weight, contract_last, preferred_element_type=jnp.float32
    )
    hidden = (jax.nn.gelu(gate_value, approximate=True) * lift_value).astype(jnp.bfloat16)
    student_all = lax.all_gather(student_in, "tensor", axis=0, tiled=True)
    row_block = hidden
    ffn_out = lax.psum_scatter(
        jnp.dot(row_block, down_weight, preferred_element_type=jnp.float32),
        "tensor",
        scatter_dimension=0,
        tiled=True,
    )
    inv_norm = lax.rsqrt(jnp.mean(ffn_out * ffn_out, axis=-1, keepdims=True) + epsilon)
    target_rows = (teacher_in.astype(jnp.float32) + ffn_out * inv_norm * gains).astype(jnp.bfloat16)
    target = lax.all_to_all(target_rows, "tensor", split_axis=1, concat_axis=0, tiled=True)
    projected = lax.dot_general(
        student_all, proj_weight, contract_last, preferred_element_type=jnp.float32
    )
    difference = projected - target.astype(jnp.float32)
    total_error = lax.psum(jnp.sum(difference * difference), "tensor")
    loss_value = total_error / (student_all.shape[0] * proj_weight.shape[0] * width_count)
    cotangent = difference.astype(jnp.bfloat16)
    proj_grad = lax.dot_general(
        cotangent, student_all, (((0,), (0,)), ((), ())), preferred_element_type=jnp.float32
    )
    row_block = cotangent
    student_grad = lax.psum_scatter(
        jnp.dot(row_block, proj_weight, preferred_element_type=jnp.float32),
        "tensor",
        scatter_dimension=0,
        tiled=True,
    ).astype(jnp.bfloat16)
    return (jnp.reshape(loss_value, (1,)), proj_grad, student_grad)


def solution(mesh):
    placed = (
        P(("groups", "tensor"), None),
        P("tensor", None),
        P("tensor", None),
        P("tensor", None),
        P(),
        P(("groups", "tensor"), None),
        P("tensor", None),
    )
    return jax.shard_map(
        local,
        mesh=mesh,
        in_specs=placed,
        out_specs=(P("groups"), P(("groups", "tensor"), None), P(("groups", "tensor"), None)),
        check_vma=False,
    )
```

profile of v0, /device:TPU:0, one launch (start us, length us, event | category | flops | bytes accessed | tf_op | source)
XLA Modules:
  0.0 371.4 jit_solution(12804801437692001570)
XLA Ops:
  7.2 0.0 copy-start
  7.2 0.0 all-gather.5.cloned.1.call-start
  7.2 0.7 all-gather.5.cloned.1.call-update
  7.9 0.0 reduce-scatter.3.cloned.1.call-start
  8.0 62.5 %all-gather.5.cloned.1.call-done = bf16[512,5376]{1,0:T(8,128)(2,1)} async-done(((bf16[32,5376]{1,0:T(8,128)(2,1)}), bf16[512,5376]{1,0:T(8,128)(2,1)}) %all-gather.5.cloned.1.call-update) | async-done | bytes 5505040 | tf_op jit(solution)/shard_map/all_gather | solution.py:13
  70.4 0.0 copy-start.3
  70.4 0.0 slice-start
  70.4 0.0 slice-start.1
  70.4 0.0 slice-start.2
  70.4 13.7 %fusion.12 = f32[512,1344]{0,1:T(8,128)} fusion(bf16[512,5376]{1,0:T(8,128)(2,1)} %all-gather.5.cloned.1.call-done, bf16[1344,5376]{1,0:T(8,128)(2,1)} %param.8), kind=kOutput, calls=%fused_computation.19 | convolution fusion | flops 7398752256 | bytes 22708224 | tf_op jit(solution)/shard_map/dot_general | solution.py:14
  84.1 0.0 copy-done.3
  84.1 0.0 slice-start.3
  84.1 11.8 %fusion = bf16[512,1344]{0,1:T(8,128)(2,1)S(1)} fusion(bf16[512,5376]{1,0:T(8,128)(2,1)S(1)} %copy-done.3, bf16[1344,5376]{1,0:T(8,128)(2,1)} %param.9, f32[512,1344]{0,1:T(8,128)} %fusion.12), kind=kOutput, calls=%fused_computation.2 | convolution fusion | flops 7405633536 | bytes 24084480 | tf_op jit(solution)/shard_map/dot_general | solution.py:17
  96.0 0.0 slice-done
  96.0 0.0 slice-done.1
  96.0 0.0 slice-done.2
  96.0 0.0 slice-done.3
  96.0 11.5 %fusion.13 = f32[512,5376]{1,0:T(8,128)} fusion(bf16[512,1344]{0,1:T(8,128)(2,1)S(1)} %fusion, bf16[1344,5376]{1,0:T(8,128)(2,1)S(1)} %bitcast.18), kind=kOutput, calls=%fused_computation.20 | convolution fusion | flops 7398752256 | bytes 26836992 | tf_op jit(solution)/shard_map/dot_general | solution.py:24
  107.5 0.0 copy-start.2
  107.5 0.0 copy-start.1
  107.5 0.0 reduce-scatter.3.cloned.1.call-update
  107.5 0.0 all-gather.3.cloned.1.call-start
  107.6 0.7 all-gather.3.cloned.1.call-update
  108.3 0.0 reduce-scatter.5.cloned.1.call-start
  108.3 0.0 copy-done.2
  108.4 120.6 %reduce-scatter.3.cloned.1.call-done = f32[32,5376]{1,0:T(8,128)} async-done(((f32[512,5376]{1,0:T(8,128)}), f32[32,5376]{1,0:T(8,128)}) %reduce-scatter.3.cloned.1.call-update) | async-done | bytes 688144 | tf_op jit(solution)/shard_map/reduce_scatter | solution.py:23
  229.0 1.3 multiply_reduce_fusion.1
  230.3 0.0 copy-done.1
  230.3 1.3 add_convert_fusion
  231.5 0.6 all_to_all.10
  232.1 0.1 copy.11
  232.2 20.2 %all_to_all.13 = bf16[32,16,336]{2,0,1:T(8,128)(2,1)S(1)} all-to-all(bf16[32,16,336]{2,0,1:T(8,128)(2,1)S(1)} %copy.11), channel_id=1, replica_groups=mesh['groups'=2,'tensor'=16] {'tensor'}, dimensions={1} | all-to-all | bytes 688128 | tf_op jit(solution)/shard_map/all_to_all | solution.py:31
  252.4 0.1 convert_element_type.37
  252.5 0.3 copy.12
  252.7 24.7 %all-gather.3.cloned.1.call-done = bf16[512,2560]{1,0:T(8,128)(2,1)} async-done(((bf16[32,2560]{1,0:T(8,128)(2,1)}), bf16[512,2560]{1,0:T(8,128)(2,1)}) %all-gather.3.cloned.1.call-update) | async-done | bytes 2621456 | tf_op jit(solution)/shard_map/all_gather | solution.py:21
  277.5 0.0 copy-done
  277.5 3.5 multiply_reduce_fusion
  281.0 3.8 %fusion.8 = f32[512,2560]{1,0:T(8,128)} fusion(bf16[336,2560]{1,0:T(8,128)(2,1)S(1)} %copy-done, bf16[512,336]{0,1:T(8,128)(2,1)S(1)} %get-tuple-element.4), kind=kOutput, calls=%fused_computation.14 | convolution fusion | flops 880803840 | bytes 7307264 | tf_op jit(solution)/shard_map/dot_general | solution.py:44
  284.9 0.0 reduce-scatter.5.cloned.1.call-update
  284.9 32.1 %psum.7 = f32[]{:T(128)} all-reduce(f32[]{:T(128)} %get-tuple-element.3), channel_id=1, replica_groups=mesh['groups'=2,'tensor'=16] {'tensor'}, use_global_device_ids=true, to_apply=%region_3.0 | all-reduce | flops 1 | bytes 8 | tf_op jit(solution)/shard_map/psum | solution.py:36
  317.6 4.6 %fusion.10 = f32[336,2560]{1,0:T(8,128)} fusion(bf16[512,2560]{1,0:T(8,128)(2,1)} %all-gather.3.cloned.1.call-done, bf16[512,336]{0,1:T(8,128)(2,1)S(1)} %get-tuple-element.4), kind=kOutput, calls=%fused_computation.16 | convolution fusion | flops 880803840 | bytes 6406144 | tf_op jit(solution)/shard_map/dot_general | solution.py:39
  322.1 40.0 %reduce-scatter.5.cloned.1.call-done = f32[32,2560]{1,0:T(8,128)} async-done(((f32[512,2560]{1,0:T(8,128)}), f32[32,2560]{1,0:T(8,128)}) %reduce-scatter.5.cloned.1.call-update) | async-done | bytes 327696 | tf_op jit(solution)/shard_map/reduce_scatter | solution.py:43
  362.1 1.7 convert_element_type.35
  (3 shorter events, 0.0 us)
Async XLA Ops:
  7.2 270.3 %copy-start = (bf16[336,2560]{1,0:T(8,128)(2,1)S(1)}, bf16[336,2560]{1,0:T(8,128)(2,1)}, u32[]{:S(2)}) copy-start(bf16[336,2560]{1,0:T(8,128)(2,1)} %param.13) | copy-start | bytes 5160964
  7.2 63.2 %all-gather.5.cloned.1.call-start = ((), (), s32[]{:S(2)}) async-start(), calls=%async_computation.4 | async-start | bytes 5849088 | tf_op jit(solution)/shard_map/all_gather | solution.py:13
  7.9 221.1 %reduce-scatter.3.cloned.1.call-start = ((), (), s32[]{:S(2)}) async-start(), calls=%async_computation.5 | async-start | bytes 11698176 | tf_op jit(solution)/shard_map/reduce_scatter | solution.py:23
  70.4 13.7 %copy-start.3 = (bf16[512,5376]{1,0:T(8,128)(2,1)S(1)}, bf16[512,5376]{1,0:T(8,128)(2,1)}, u32[]{:S(2)}) copy-start(bf16[512,5376]{1,0:T(8,128)(2,1)} %all-gather.5.cloned.1.call-done) | copy-start | bytes 16515076
  70.4 25.6 %slice-start = ((s8[14450688]{0:T(1024)(128)(4,1)}), s8[4194304]{0:T(1024)(128)(4,1)S(1)}, s32[]{:S(2)}) async-start(s8[14450688]{0:T(1024)(128)(4,1)} %bitcast.17), calls=%async_computation.7 | async-start | bytes 8388608
  70.4 25.6 %slice-start.1 = ((s8[14450688]{0:T(1024)(128)(4,1)}), s8[4194304]{0:T(1024)(128)(4,1)S(1)}, s32[]{:S(2)}) async-start(s8[14450688]{0:T(1024)(128)(4,1)} %bitcast.17), calls=%async_computation.8 | async-start | bytes 8388608
  70.4 25.6 %slice-start.2 = ((s8[14450688]{0:T(1024)(128)(4,1)}), s8[4194304]{0:T(1024)(128)(4,1)S(1)}, s32[]{:S(2)}) async-start(s8[14450688]{0:T(1024)(128)(4,1)} %bitcast.17), calls=%async_computation.9 | async-start | bytes 8388608
  84.1 11.9 %slice-start.3 = ((s8[14450688]{0:T(1024)(128)(4,1)}), s8[1867776]{0:T(1024)(128)(4,1)S(1)}, s32[]{:S(2)}) async-start(s8[14450688]{0:T(1024)(128)(4,1)} %bitcast.17), calls=%async_computation.10 | async-start | bytes 3735552
  107.5 0.8 copy-start.2
  107.5 122.7 %copy-start.1 = (bf16[32,5376]{1,0:T(8,128)(2,1)S(1)}, bf16[32,5376]{1,0:T(8,128)(2,1)}, u32[]{:S(2)}) copy-start(bf16[32,5376]{1,0:T(8,128)(2,1)} %param.7) | copy-start | bytes 1032196
  107.5 169.9 %all-gather.3.cloned.1.call-start = ((), (), s32[]{:S(2)}) async-start(), calls=%async_computation.3 | async-start | bytes 2785280 | tf_op jit(solution)/shard_map/all_gather | solution.py:21
  108.3 253.8 %reduce-scatter.5.cloned.1.call-start = ((), (), s32[]{:S(2)}) async-start(), calls=%async_computation.6 | async-start | bytes 5570560 | tf_op jit(solution)/shard_map/reduce_scatter | solution.py:43
Sparse Core Ops, SparseCore 0:
  10.3 60.0 all-gather.4
  107.7 121.2 reduce-scatter.2
  231.5 45.8 all-gather.2
  285.0 77.0 reduce-scatter.4
where the time goes:
time: 372 us; the launch traced here: 371 us
  waiting for transfers between devices  249 us (67%)
  blocking collectives  52.2 us (14%)
  matrix products  48.9 us (13%)
  between operations  15.7 us (4%)
  other arithmetic  4.27 us (1%)
    reduce_scatter x1, waiting for transfers between devices, local(): lax.psum_scatter(jnp.dot(row_block, down_weight, preferred_element_type=j...  121 us
    all_gather x1, waiting for transfers between devices, local(): block_rows = lax.all_gather(teacher_in, 'tensor', axis=0, tiled=True)  62.5 us
    reduce_scatter x1, waiting for transfers between devices, local(): lax.psum_scatter(jnp.dot(row_block, proj_weight, preferred_element_type=j...  40 us
    psum x1, blocking collectives, local(): total_error = lax.psum(jnp.sum(difference * difference), 'tensor')  32.1 us
    all_gather x1, waiting for transfers between devices, local(): student_all = lax.all_gather(student_in, 'tensor', axis=0, tiled=True)  24.7 us
    all_to_all x1, blocking collectives, local(): lax.all_to_all(target_rows, 'tensor', split_axis=1, concat_axis=0, tiled=...  20.2 us
    dot_general x1, matrix products, local(): lax.dot_general(block_rows, gate_weight, contract_last, preferred_element...  13.7 us
    dot_general x1, matrix products, local(): lax.dot_general(block_rows, up_weight, contract_last, preferred_element_t...  11.8 us
  transfers between devices with their start and end apart: 4, of which 4 were waited for; matrix products, arithmetic and copies ran while one was open for 2% of the time, Pallas kernels for 0%

commit v1 on v0

--- a/solution.py
+++ b/solution.py
@@ -6,11 +6,23 @@
 epsilon = 1e-06
 
 
+def edit_stocks_on_mesh(x0):
+    mixed_arr, z, r1 = (lax.axis_size("tensor"), lax.axis_index("tensor"), x0.shape[0])
+    pieces_in = [tick * mixed_arr if dd == 0 else tick for dd, tick in enumerate(x0.shape)]
+    extra = lax.dynamic_update_slice_in_dim(jnp.zeros(pieces_in, x0.dtype), x0, z * r1, axis=0)
+    for at in range(1, mixed_arr):
+        x0 = lax.ppermute(
+            x0, "tensor", list(map(lambda dd: (dd, (dd + 1) % mixed_arr), range(mixed_arr)))
+        )
+        extra = lax.dynamic_update_slice_in_dim(extra, x0, (z - at) % mixed_arr * r1, axis=0)
+    return extra
+
+
 def local(teacher_in, gate_weight, up_weight, down_weight, post_gain, student_in, proj_weight):
     width_count = lax.axis_size("tensor")
     gains = post_gain.astype(jnp.float32)
     contract_last = (((1,), (1,)), ((), ()))
-    block_rows = lax.all_gather(teacher_in, "tensor", axis=0, tiled=True)
+    block_rows = edit_stocks_on_mesh(teacher_in)
     gate_value = lax.dot_general(
         block_rows, gate_weight, contract_last, preferred_element_type=jnp.float32
     )

time: 372 us -> 449 us (1.21)
  waiting for transfers between devices: 249 us -> 325 us
    ppermute x0 -> x15, waiting for transfers between devices: none -> 140 us  [edit_stocks_on_mesh(): lax.ppermute(x0, 'tensor', list(map(lambda dd: (dd, (dd + 1) % mixed_arr)...]
    all_gather x1 -> x0, waiting for transfers between devices: 62.5 us -> none  [local(): block_rows = lax.all_gather(teacher_in, 'tensor', axis=0, tiled=True)]
  transfers between devices with their start and end apart: 4 -> 18, of which waited for: 4 -> 18; matrix products, arithmetic and copies ran while one was open for 2% -> 2% of each run, Pallas kernels for 0% -> 0%
where the time goes in v1:
time: 449 us
  waiting for transfers between devices  325 us (72%)
  blocking collectives  52.3 us (12%)
  matrix products  48.6 us (11%)
  between operations  15.7 us (3%)
    ppermute x15, waiting for transfers between devices, edit_stocks_on_mesh(): lax.ppermute(x0, 'tensor', list(map(lambda dd: (dd, (dd + 1) % mixed_arr)...  140 us
    reduce_scatter x1, waiting for transfers between devices, local(): lax.psum_scatter(jnp.dot(row_block, down_weight, preferred_element_type=j...  120 us
    reduce_scatter x1, waiting for transfers between devices, local(): lax.psum_scatter(jnp.dot(row_block, proj_weight, preferred_element_type=j...  39.9 us
    psum x1, blocking collectives, local(): total_error = lax.psum(jnp.sum(difference * difference), 'tensor')  32.1 us
    all_gather x1, waiting for transfers between devices, local(): student_all = lax.all_gather(student_in, 'tensor', axis=0, tiled=True)  24.7 us
    all_to_all x1, blocking collectives, local(): lax.all_to_all(target_rows, 'tensor', split_axis=1, concat_axis=0, tiled=...  20.2 us
    dot_general x1, matrix products, local(): jnp.dot(row_block, down_weight, preferred_element_type=jnp.float32)  13.9 us
    dot_general x1, matrix products, local(): lax.dot_general(block_rows, up_weight, contract_last, preferred_element_t...  12.1 us
  transfers between devices with their start and end apart: 18, of which 18 were waited for; matrix products, arithmetic and copies ran while one was open for 2% of the time, Pallas kernels for 0%

profile of v1, /device:TPU:0, one launch (start us, length us, event | category | flops | bytes accessed | tf_op | source)
XLA Modules:
  0.0 448.9 jit_solution(9977629862394994753)
XLA Ops:
  7.2 0.0 copy-start
  7.2 0.0 reduce-scatter.3.cloned.1.call-start
  7.2 0.5 collective-permute-start
  7.7 0.4 broadcast_in_dim.2
  8.1 0.2 copy-done.1
  8.3 9.6 %collective-permute-done = bf16[32,5376]{1,0:T(8,128)(2,1)S(1)} collective-permute-done((bf16[32,5376]{1,0:T(8,128)(2,1)}, bf16[32,5376]{1,0:T(8,128)(2,1)S(1)}, u32[]{:S(2)}, u32[]{:S(2)}) %collective-permute-start) | collective-permute-done | bytes 344096 | tf_op jit(solution)/shard_map/ppermute | solution.py:14
  17.9 0.0 collective-permute-start.1
  17.9 9.3 %collective-permute-done.1 = bf16[32,5376]{1,0:T(8,128)(2,1)S(1)} collective-permute-done((bf16[32,5376]{1,0:T(8,128)(2,1)S(1)}, bf16[32,5376]{1,0:T(8,128)(2,1)S(1)}, u32[]{:S(2)}, u32[]{:S(2)}) %collective-permute-start.1) | collective-permute-done | bytes 344096 | tf_op jit(solution)/shard_map/ppermute | solution.py:14
  27.3 9.3 %collective-permute-done.2 = bf16[32,5376]{1,0:T(8,128)(2,1)S(1)} collective-permute-done((bf16[32,5376]{1,0:T(8,128)(2,1)S(1)}, bf16[32,5376]{1,0:T(8,128)(2,1)S(1)}, u32[]{:S(2)}, u32[]{:S(2)}) %collective-permute-start.2) | collective-permute-done | bytes 344096 | tf_op jit(solution)/shard_map/ppermute | solution.py:14
  36.6 0.0 collective-permute-start.3
  36.7 9.3 %collective-permute-done.3 = bf16[32,5376]{1,0:T(8,128)(2,1)S(1)} collective-permute-done((bf16[32,5376]{1,0:T(8,128)(2,1)S(1)}, bf16[32,5376]{1,0:T(8,128)(2,1)S(1)}, u32[]{:S(2)}, u32[]{:S(2)}) %collective-permute-start.3) | collective-permute-done | bytes 344096 | tf_op jit(solution)/shard_map/ppermute | solution.py:14
  46.0 9.3 %collective-permute-done.4 = bf16[32,5376]{1,0:T(8,128)(2,1)S(1)} collective-permute-done((bf16[32,5376]{1,0:T(8,128)(2,1)S(1)}, bf16[32,5376]{1,0:T(8,128)(2,1)S(1)}, u32[]{:S(2)}, u32[]{:S(2)}) %collective-permute-start.4) | collective-permute-done | bytes 344096 | tf_op jit(solution)/shard_map/ppermute | solution.py:14
  55.4 9.3 %collective-permute-done.5 = bf16[32,5376]{1,0:T(8,128)(2,1)S(1)} collective-permute-done((bf16[32,5376]{1,0:T(8,128)(2,1)S(1)}, bf16[32,5376]{1,0:T(8,128)(2,1)S(1)}, u32[]{:S(2)}, u32[]{:S(2)}) %collective-permute-start.5) | collective-permute-done | bytes 344096 | tf_op jit(solution)/shard_map/ppermute | solution.py:14
  64.8 9.3 %collective-permute-done.6 = bf16[32,5376]{1,0:T(8,128)(2,1)S(1)} collective-permute-done((bf16[32,5376]{1,0:T(8,128)(2,1)S(1)}, bf16[32,5376]{1,0:T(8,128)(2,1)S(1)}, u32[]{:S(2)}, u32[]{:S(2)}) %collective-permute-start.6) | collective-permute-done | bytes 344096 | tf_op jit(solution)/shard_map/ppermute | solution.py:14
  74.1 9.3 %collective-permute-done.7 = bf16[32,5376]{1,0:T(8,128)(2,1)S(1)} collective-permute-done((bf16[32,5376]{1,0:T(8,128)(2,1)S(1)}, bf16[32,5376]{1,0:T(8,128)(2,1)S(1)}, u32[]{:S(2)}, u32[]{:S(2)}) %collective-permute-start.7) | collective-permute-done | bytes 344096 | tf_op jit(solution)/shard_map/ppermute | solution.py:14
  83.5 9.3 %collective-permute-done.8 = bf16[32,5376]{1,0:T(8,128)(2,1)S(1)} collective-permute-done((bf16[32,5376]{1,0:T(8,128)(2,1)S(1)}, bf16[32,5376]{1,0:T(8,128)(2,1)S(1)}, u32[]{:S(2)}, u32[]{:S(2)}) %collective-permute-start.8) | collective-permute-done | bytes 344096 | tf_op jit(solution)/shard_map/ppermute | solution.py:14
  92.9 9.3 %collective-permute-done.9 = bf16[32,5376]{1,0:T(8,128)(2,1)S(1)} collective-permute-done((bf16[32,5376]{1,0:T(8,128)(2,1)S(1)}, bf16[32,5376]{1,0:T(8,128)(2,1)S(1)}, u32[]{:S(2)}, u32[]{:S(2)}) %collective-permute-start.9) | collective-permute-done | bytes 344096 | tf_op jit(solution)/shard_map/ppermute | solution.py:14
  102.3 9.3 %collective-permute-done.10 = bf16[32,5376]{1,0:T(8,128)(2,1)S(1)} collective-permute-done((bf16[32,5376]{1,0:T(8,128)(2,1)S(1)}, bf16[32,5376]{1,0:T(8,128)(2,1)S(1)}, u32[]{:S(2)}, u32[]{:S(2)}) %collective-permute-start.10) | collective-permute-done | bytes 344096 | tf_op jit(solution)/shard_map/ppermute | solution.py:14
  111.6 9.3 %collective-permute-done.11 = bf16[32,5376]{1,0:T(8,128)(2,1)S(1)} collective-permute-done((bf16[32,5376]{1,0:T(8,128)(2,1)S(1)}, bf16[32,5376]{1,0:T(8,128)(2,1)S(1)}, u32[]{:S(2)}, u32[]{:S(2)}) %collective-permute-start.11) | collective-permute-done | bytes 344096 | tf_op jit(solution)/shard_map/ppermute | solution.py:14
  121.0 9.3 %collective-permute-done.12 = bf16[32,5376]{1,0:T(8,128)(2,1)S(1)} collective-permute-done((bf16[32,5376]{1,0:T(8,128)(2,1)S(1)}, bf16[32,5376]{1,0:T(8,128)(2,1)S(1)}, u32[]{:S(2)}, u32[]{:S(2)}) %collective-permute-start.12) | collective-permute-done | bytes 344096 | tf_op jit(solution)/shard_map/ppermute | solution.py:14
  130.4 9.3 %collective-permute-done.13 = bf16[32,5376]{1,0:T(8,128)(2,1)S(1)} collective-permute-done((bf16[32,5376]{1,0:T(8,128)(2,1)S(1)}, bf16[32,5376]{1,0:T(8,128)(2,1)S(1)}, u32[]{:S(2)}, u32[]{:S(2)}) %collective-permute-start.13) | collective-permute-done | bytes 344096 | tf_op jit(solution)/shard_map/ppermute | solution.py:14
  139.8 9.3 %collective-permute-done.14 = bf16[32,5376]{1,0:T(8,128)(2,1)S(1)} collective-permute-done((bf16[32,5376]{1,0:T(8,128)(2,1)S(1)}, bf16[32,5376]{1,0:T(8,128)(2,1)S(1)}, u32[]{:S(2)}, u32[]{:S(2)}) %collective-permute-start.14) | collective-permute-done | bytes 344096 | tf_op jit(solution)/shard_map/ppermute | solution.py:14
  149.1 0.0 slice-start
  149.1 0.0 slice-start.1
  149.1 10.6 %fusion.23 = f32[512,1344]{0,1:T(8,128)S(1)} fusion(bf16[512,5376]{1,0:T(8,128)(2,1)S(1)} %constant_dynamic-update-slice_fusion, bf16[1344,5376]{1,0:T(8,128)(2,1)} %param.8), kind=kOutput, calls=%fused_computation.44 | convolution fusion | flops 7398752256 | bytes 22708224 | tf_op jit(solution)/shard_map/dot_general | solution.py:26
  159.7 0.0 slice-start.2
  159.8 12.1 %fusion.24 = f32[512,1344]{0,1:T(8,128)} fusion(bf16[512,5376]{1,0:T(8,128)(2,1)S(1)} %constant_dynamic-update-slice_fusion, bf16[1344,5376]{1,0:T(8,128)(2,1)} %param.9), kind=kOutput, calls=%fused_computation.45 | convolution fusion | flops 7398752256 | bytes 22708224 | tf_op jit(solution)/shard_map/dot_general | solution.py:29
  171.9 13.9 %fusion.9 = f32[512,5376]{1,0:T(8,128)} fusion(bf16[1344,5376]{1,0:T(8,128)(2,1)S(1)} %bitcast.16, f32[512,1344]{0,1:T(8,128)} %fusion.24, f32[512,1344]{0,1:T(8,128)S(1)} %fusion.23), kind=kOutput, calls=%fused_computation.10 | convolution fusion | flops 7405633536 | bytes 30965760 | tf_op jit(solution)/shard_map/dot_general | solution.py:36
  185.9 0.0 reduce-scatter.3.cloned.1.call-update
  185.9 0.0 all-gather.2.cloned.1.call-start
  185.9 0.7 all-gather.2.cloned.1.call-update
  186.6 0.2 reduce-scatter.5.cloned.1.call-start
  186.9 119.6 %reduce-scatter.3.cloned.1.call-done = f32[32,5376]{1,0:T(8,128)} async-done(((f32[512,5376]{1,0:T(8,128)}), f32[32,5376]{1,0:T(8,128)}) %reduce-scatter.3.cloned.1.call-update) | async-done | bytes 688144 | tf_op jit(solution)/shard_map/reduce_scatter | solution.py:35
  306.4 1.3 multiply_reduce_fusion.1
  307.7 1.3 add_convert_fusion
  309.0 0.6 all_to_all.10
  309.6 0.1 copy.11
  309.7 20.2 %all_to_all.13 = bf16[32,16,336]{2,0,1:T(8,128)(2,1)S(1)} all-to-all(bf16[32,16,336]{2,0,1:T(8,128)(2,1)S(1)} %copy.11), channel_id=1, replica_groups=mesh['groups'=2,'tensor'=16] {'tensor'}, dimensions={1} | all-to-all | bytes 688128 | tf_op jit(solution)/shard_map/all_to_all | solution.py:43
  329.9 0.1 convert_element_type.37
  330.0 0.3 copy.12
  330.2 24.7 %all-gather.2.cloned.1.call-done = bf16[512,2560]{1,0:T(8,128)(2,1)} async-done(((bf16[32,2560]{1,0:T(8,128)(2,1)}), bf16[512,2560]{1,0:T(8,128)(2,1)}) %all-gather.2.cloned.1.call-update) | async-done | bytes 2621456 | tf_op jit(solution)/shard_map/all_gather | solution.py:33
  354.9 3.5 multiply_reduce_fusion
  358.5 3.9 fusion.15
  362.3 0.0 reduce-scatter.5.cloned.1.call-update
  362.4 32.1 %psum.7 = f32[]{:T(128)} all-reduce(f32[]{:T(128)} %get-tuple-element.3), channel_id=1, replica_groups=mesh['groups'=2,'tensor'=16] {'tensor'}, use_global_device_ids=true, to_apply=%region_3.4 | all-reduce | flops 1 | bytes 8 | tf_op jit(solution)/shard_map/psum | solution.py:48
  395.1 4.6 %fusion.17 = f32[336,2560]{1,0:T(8,128)} fusion(bf16[512,2560]{1,0:T(8,128)(2,1)} %all-gather.2.cloned.1.call-done, bf16[512,336]{0,1:T(8,128)(2,1)S(1)} %get-tuple-element.4), kind=kOutput, calls=%fused_computation.21 | convolution fusion | flops 880803840 | bytes 6406144 | tf_op jit(solution)/shard_map/dot_general | solution.py:51
  399.6 39.9 %reduce-scatter.5.cloned.1.call-done = f32[32,2560]{1,0:T(8,128)} async-done(((f32[512,2560]{1,0:T(8,128)}), f32[32,2560]{1,0:T(8,128)}) %reduce-scatter.5.cloned.1.call-update) | async-done | bytes 327696 | tf_op jit(solution)/shard_map/reduce_scatter | solution.py:55
  439.6 1.7 convert_element_type.35
  (40 shorter events, 0.5 us)
Async XLA Ops:
  7.2 347.8 %copy-start = (bf16[336,2560]{1,0:T(8,128)(2,1)S(1)}, bf16[336,2560]{1,0:T(8,128)(2,1)}, u32[]{:S(2)}) copy-start(bf16[336,2560]{1,0:T(8,128)(2,1)} %param.13) | copy-start | bytes 5160964
  7.2 1.1 copy-start.1
  7.2 299.3 %reduce-scatter.3.cloned.1.call-start = ((), (), s32[]{:S(2)}) async-start(), calls=%async_computation.4 | async-start | bytes 11698176 | tf_op jit(solution)/shard_map/reduce_scatter | solution.py:35
  7.2 10.6 %collective-permute-start = (bf16[32,5376]{1,0:T(8,128)(2,1)}, bf16[32,5376]{1,0:T(8,128)(2,1)S(1)}, u32[]{:S(2)}, u32[]{:S(2)}) collective-permute-start(bf16[32,5376]{1,0:T(8,128)(2,1)} %param.7), channel_id=1, source_target_pairs={{0,1},{1,2},{2,3},{3,4},{4,5},{5,6},{6,7},{7,8},{8,9},{9,10},{10,1... | collective-permute-start | bytes 1032200 | tf_op jit(solution)/shard_map/ppermute | solution.py:14
  17.9 9.4 %collective-permute-start.1 = (bf16[32,5376]{1,0:T(8,128)(2,1)S(1)}, bf16[32,5376]{1,0:T(8,128)(2,1)S(1)}, u32[]{:S(2)}, u32[]{:S(2)}) collective-permute-start(bf16[32,5376]{1,0:T(8,128)(2,1)S(1)} %collective-permute-done), channel_id=1, source_target_pairs={{0,1},{1,2},{2,3},{3,4},{4,5},{5,6},{6,7},{7,8},{8,9},{9,10},{10,1... | collective-permute-start | bytes 1032200 | tf_op jit(solution)/shard_map/ppermute | solution.py:14
  27.2 9.4 %collective-permute-start.2 = (bf16[32,5376]{1,0:T(8,128)(2,1)S(1)}, bf16[32,5376]{1,0:T(8,128)(2,1)S(1)}, u32[]{:S(2)}, u32[]{:S(2)}) collective-permute-start(bf16[32,5376]{1,0:T(8,128)(2,1)S(1)} %collective-permute-done.1), channel_id=1, source_target_pairs={{0,1},{1,2},{2,3},{3,4},{4,5},{5,6},{6,7},{7,8},{8,9},{9,10},{10,1... | collective-permute-start | bytes 1032200 | tf_op jit(solution)/shard_map/ppermute | solution.py:14
  36.6 9.4 %collective-permute-start.3 = (bf16[32,5376]{1,0:T(8,128)(2,1)S(1)}, bf16[32,5376]{1,0:T(8,128)(2,1)S(1)}, u32[]{:S(2)}, u32[]{:S(2)}) collective-permute-start(bf16[32,5376]{1,0:T(8,128)(2,1)S(1)} %collective-permute-done.2), channel_id=1, source_target_pairs={{0,1},{1,2},{2,3},{3,4},{4,5},{5,6},{6,7},{7,8},{8,9},{9,10},{10,1... | collective-permute-start | bytes 1032200 | tf_op jit(solution)/shard_map/ppermute | solution.py:14
  46.0 9.4 %collective-permute-start.4 = (bf16[32,5376]{1,0:T(8,128)(2,1)S(1)}, bf16[32,5376]{1,0:T(8,128)(2,1)S(1)}, u32[]{:S(2)}, u32[]{:S(2)}) collective-permute-start(bf16[32,5376]{1,0:T(8,128)(2,1)S(1)} %collective-permute-done.3), channel_id=1, source_target_pairs={{0,1},{1,2},{2,3},{3,4},{4,5},{5,6},{6,7},{7,8},{8,9},{9,10},{10,1... | collective-permute-start | bytes 1032200 | tf_op jit(solution)/shard_map/ppermute | solution.py:14
  55.4 9.4 %collective-permute-start.5 = (bf16[32,5376]{1,0:T(8,128)(2,1)S(1)}, bf16[32,5376]{1,0:T(8,128)(2,1)S(1)}, u32[]{:S(2)}, u32[]{:S(2)}) collective-permute-start(bf16[32,5376]{1,0:T(8,128)(2,1)S(1)} %collective-permute-done.4), channel_id=1, source_target_pairs={{0,1},{1,2},{2,3},{3,4},{4,5},{5,6},{6,7},{7,8},{8,9},{9,10},{10,1... | collective-permute-start | bytes 1032200 | tf_op jit(solution)/shard_map/ppermute | solution.py:14
  64.7 9.4 %collective-permute-start.6 = (bf16[32,5376]{1,0:T(8,128)(2,1)S(1)}, bf16[32,5376]{1,0:T(8,128)(2,1)S(1)}, u32[]{:S(2)}, u32[]{:S(2)}) collective-permute-start(bf16[32,5376]{1,0:T(8,128)(2,1)S(1)} %collective-permute-done.5), channel_id=1, source_target_pairs={{0,1},{1,2},{2,3},{3,4},{4,5},{5,6},{6,7},{7,8},{8,9},{9,10},{10,1... | collective-permute-start | bytes 1032200 | tf_op jit(solution)/shard_map/ppermute | solution.py:14
  74.1 9.4 %collective-permute-start.7 = (bf16[32,5376]{1,0:T(8,128)(2,1)S(1)}, bf16[32,5376]{1,0:T(8,128)(2,1)S(1)}, u32[]{:S(2)}, u32[]{:S(2)}) collective-permute-start(bf16[32,5376]{1,0:T(8,128)(2,1)S(1)} %collective-permute-done.6), channel_id=1, source_target_pairs={{0,1},{1,2},{2,3},{3,4},{4,5},{5,6},{6,7},{7,8},{8,9},{9,10},{10,1... | collective-permute-start | bytes 1032200 | tf_op jit(solution)/shard_map/ppermute | solution.py:14
  83.5 9.4 %collective-permute-start.8 = (bf16[32,5376]{1,0:T(8,128)(2,1)S(1)}, bf16[32,5376]{1,0:T(8,128)(2,1)S(1)}, u32[]{:S(2)}, u32[]{:S(2)}) collective-permute-start(bf16[32,5376]{1,0:T(8,128)(2,1)S(1)} %collective-permute-done.7), channel_id=1, source_target_pairs={{0,1},{1,2},{2,3},{3,4},{4,5},{5,6},{6,7},{7,8},{8,9},{9,10},{10,1... | collective-permute-start | bytes 1032200 | tf_op jit(solution)/shard_map/ppermute | solution.py:14
  92.9 9.4 %collective-permute-start.9 = (bf16[32,5376]{1,0:T(8,128)(2,1)S(1)}, bf16[32,5376]{1,0:T(8,128)(2,1)S(1)}, u32[]{:S(2)}, u32[]{:S(2)}) collective-permute-start(bf16[32,5376]{1,0:T(8,128)(2,1)S(1)} %collective-permute-done.8), channel_id=1, source_target_pairs={{0,1},{1,2},{2,3},{3,4},{4,5},{5,6},{6,7},{7,8},{8,9},{9,10},{10,1... | collective-permute-start | bytes 1032200 | tf_op jit(solution)/shard_map/ppermute | solution.py:14
  102.2 9.4 %collective-permute-start.10 = (bf16[32,5376]{1,0:T(8,128)(2,1)S(1)}, bf16[32,5376]{1,0:T(8,128)(2,1)S(1)}, u32[]{:S(2)}, u32[]{:S(2)}) collective-permute-start(bf16[32,5376]{1,0:T(8,128)(2,1)S(1)} %collective-permute-done.9), channel_id=1, source_target_pairs={{0,1},{1,2},{2,3},{3,4},{4,5},{5,6},{6,7},{7,8},{8,9},{9,10},{10,1... | collective-permute-start | bytes 1032200 | tf_op jit(solution)/shard_map/ppermute | solution.py:14
  111.6 9.4 %collective-permute-start.11 = (bf16[32,5376]{1,0:T(8,128)(2,1)S(1)}, bf16[32,5376]{1,0:T(8,128)(2,1)S(1)}, u32[]{:S(2)}, u32[]{:S(2)}) collective-permute-start(bf16[32,5376]{1,0:T(8,128)(2,1)S(1)} %collective-permute-done.10), channel_id=1, source_target_pairs={{0,1},{1,2},{2,3},{3,4},{4,5},{5,6},{6,7},{7,8},{8,9},{9,10},{10,1... | collective-permute-start | bytes 1032200 | tf_op jit(solution)/shard_map/ppermute | solution.py:14
  121.0 9.4 %collective-permute-start.12 = (bf16[32,5376]{1,0:T(8,128)(2,1)S(1)}, bf16[32,5376]{1,0:T(8,128)(2,1)S(1)}, u32[]{:S(2)}, u32[]{:S(2)}) collective-permute-start(bf16[32,5376]{1,0:T(8,128)(2,1)S(1)} %collective-permute-done.11), channel_id=1, source_target_pairs={{0,1},{1,2},{2,3},{3,4},{4,5},{5,6},{6,7},{7,8},{8,9},{9,10},{10,1... | collective-permute-start | bytes 1032200 | tf_op jit(solution)/shard_map/ppermute | solution.py:14
  130.3 9.4 %collective-permute-start.13 = (bf16[32,5376]{1,0:T(8,128)(2,1)S(1)}, bf16[32,5376]{1,0:T(8,128)(2,1)S(1)}, u32[]{:S(2)}, u32[]{:S(2)}) collective-permute-start(bf16[32,5376]{1,0:T(8,128)(2,1)S(1)} %collective-permute-done.12), channel_id=1, source_target_pairs={{0,1},{1,2},{2,3},{3,4},{4,5},{5,6},{6,7},{7,8},{8,9},{9,10},{10,1... | collective-permute-start | bytes 1032200 | tf_op jit(solution)/shard_map/ppermute | solution.py:14
  139.7 9.4 %collective-permute-start.14 = (bf16[32,5376]{1,0:T(8,128)(2,1)S(1)}, bf16[32,5376]{1,0:T(8,128)(2,1)S(1)}, u32[]{:S(2)}, u32[]{:S(2)}) collective-permute-start(bf16[32,5376]{1,0:T(8,128)(2,1)S(1)} %collective-permute-done.13), channel_id=1, source_target_pairs={{0,1},{1,2},{2,3},{3,4},{4,5},{5,6},{6,7},{7,8},{8,9},{9,10},{10,1... | collective-permute-start | bytes 1032200 | tf_op jit(solution)/shard_map/ppermute | solution.py:14
  149.1 22.8 %slice-start = ((s8[14450688]{0:T(1024)(128)(4,1)}), s8[4194304]{0:T(1024)(128)(4,1)S(1)}, s32[]{:S(2)}) async-start(s8[14450688]{0:T(1024)(128)(4,1)} %bitcast.15), calls=%async_computation.6 | async-start | bytes 8388608
  149.1 22.8 %slice-start.1 = ((s8[14450688]{0:T(1024)(128)(4,1)}), s8[4194304]{0:T(1024)(128)(4,1)S(1)}, s32[]{:S(2)}) async-start(s8[14450688]{0:T(1024)(128)(4,1)} %bitcast.15), calls=%async_computation.7 | async-start | bytes 8388608
  159.7 12.2 %slice-start.2 = ((s8[14450688]{0:T(1024)(128)(4,1)}), s8[4194304]{0:T(1024)(128)(4,1)S(1)}, s32[]{:S(2)}) async-start(s8[14450688]{0:T(1024)(128)(4,1)} %bitcast.15), calls=%async_computation.8 | async-start | bytes 8388608
  159.8 12.2 %slice-start.3 = ((s8[14450688]{0:T(1024)(128)(4,1)}), s8[1867776]{0:T(1024)(128)(4,1)S(1)}, s32[]{:S(2)}) async-start(s8[14450688]{0:T(1024)(128)(4,1)} %bitcast.15), calls=%async_computation.9 | async-start | bytes 3735552
  185.8 1.0 copy-start.2
  185.9 169.1 %all-gather.2.cloned.1.call-start = ((), (), s32[]{:S(2)}) async-start(), calls=%async_computation.3 | async-start | bytes 2785280 | tf_op jit(solution)/shard_map/all_gather | solution.py:33
  186.6 252.9 %reduce-scatter.5.cloned.1.call-start = ((), (), s32[]{:S(2)}) async-start(), calls=%async_computation.5 | async-start | bytes 5570560 | tf_op jit(solution)/shard_map/reduce_scatter | solution.py:55
Sparse Core Ops, SparseCore 0:
  186.0 120.4 reduce-scatter.2
  309.0 45.9 all-gather.1
  362.5 77.0 reduce-scatter.4
